TPU v7x, 32 devices: a whole 2x2x4 slice. The times are simulated.
32 devices in a mesh: fsdp: 4 (over z), ctx: 2 (over x), tp: 4 (over y, core).
Axes of the slice: x: 2, y: 2, z: 4, core: 2. Of those that a mesh axis runs over, the one named last changes fastest.
Arguments:
- tokens: bfloat16 [8, 1024, 1024], P('fsdp', ('ctx', 'tp')), may hold values from -6 to 6
- key_valid: int32 [8, 1024], P('fsdp'), may hold values from 0 to 1, as said below
- first_gain: bfloat16 [2, 1024], P(None, 'fsdp'), may hold values from 0.25 to 1.75
- first_shift: bfloat16 [2, 1024], P(None, 'fsdp'), may hold values from -1.75 to 1.75
- joint_weight: bfloat16 [2, 1024, 3, 1024], P(None, 'fsdp', None, 'tp'), may hold values from -0.1875 to 0.1875
- query_bias: bfloat16 [2, 16, 64], P(None, 'tp', 'fsdp'), may hold values from -3 to 3
- value_bias: bfloat16 [2, 16, 64], P(None, 'tp', 'fsdp'), may hold values from -0.625 to 0.625
- out_weight: bfloat16 [2, 1024, 1024], P(None, 'tp', 'fsdp'), may hold values from -0.75 to 0.75
- out_bias: bfloat16 [2, 1024], P(None, 'fsdp'), may hold values from -1.75 to 1.75
- second_gain: bfloat16 [2, 1024], P(None, 'fsdp'), may hold values from 0.25 to 1.75
- second_shift: bfloat16 [2, 1024], P(None, 'fsdp'), may hold values from -1.75 to 1.75
- expand_weight: bfloat16 [2, 1024, 4096], P(None, 'fsdp', 'tp'), may hold values from -0.1875 to 0.1875
- expand_bias: bfloat16 [2, 64, 64], P(None, 'tp', 'fsdp'), may hold values from -3 to 3
- reduce_weight: bfloat16 [2, 4096, 1024], P(None, 'tp', 'fsdp'), may hold values from -0.09375 to 0.09375
- reduce_bias: bfloat16 [2, 1024], P(None, 'fsdp'), may hold values from -1.75 to 1.75
- cotangent: bfloat16 [8, 1024, 1024], P('fsdp', ('ctx', 'tp')), may hold values from -6 to 6
Outputs:
- output: bfloat16 [8, 1024, 1024], P('fsdp', ('ctx', 'tp'))
- input_grad: bfloat16 [8, 1024, 1024], P('fsdp', ('ctx', 'tp'))
- grad_first_gain: float32 [2, 1024], P(None, 'fsdp')
- grad_first_shift: float32 [2, 1024], P(None, 'fsdp')
- grad_joint_weight: float32 [2, 1024, 3, 1024], P(None, 'fsdp', None, 'tp')
- grad_query_bias: float32 [2, 16, 64], P(None, 'tp', 'fsdp')
- grad_value_bias: float32 [2, 16, 64], P(None, 'tp', 'fsdp')
- grad_out_weight: float32 [2, 1024, 1024], P(None, 'tp', 'fsdp')
- grad_out_bias: float32 [2, 1024], P(None, 'fsdp')
- grad_second_gain: float32 [2, 1024], P(None, 'fsdp')
- grad_second_shift: float32 [2, 1024], P(None, 'fsdp')
- grad_expand_weight: float32 [2, 1024, 4096], P(None, 'fsdp', 'tp')
- grad_expand_bias: float32 [2, 64, 64], P(None, 'tp', 'fsdp')
- grad_reduce_weight: float32 [2, 4096, 1024], P(None, 'tp', 'fsdp')
- grad_reduce_bias: float32 [2, 1024], P(None, 'fsdp')
Inputs may be any that keep to these rules, and one draw needn't show every extreme that they name: `key_valid`: in each clip the ones form a prefix of 128 tokens or more; clip 0 has ones throughout.
All inputs are finite; a program needn't handle non-finite values.
Results may differ from a plain program's by a relative error of at most 0.02.
Values may be sent and summed in bfloat16 or wider, within the bound.
A program may use at most 256 MiB of HBM per device.

v0:
```python
import jax
import jax.numpy as jnp
from jax import lax
from jax.sharding import PartitionSpec as P

HD = 64
LAYERS = 2
MB = 2
epsilon = 1e-06
masked_score = -10000.0


def norm_rows(rows, gain, shift):
    middle = jnp.mean(rows, axis=-1, keepdims=True)
    centred = rows - middle
    spread = jnp.mean(centred * centred, axis=-1, keepdims=True)
    return centred * lax.rsqrt(spread + epsilon) * gain + shift


def exact_gelu(values):
    return jax.nn.gelu(values, approximate=False)


def dense(left, right):
    return jnp.dot(left, right, preferred_element_type=jnp.float32)


def dense_left(left, right):
    return lax.dot_general(
        left, right, (((0,), (0,)), ((), ())), preferred_element_type=jnp.float32
    )


def dense_right(left, right):
    return lax.dot_general(
        left, right, (((1,), (1,)), ((), ())), preferred_element_type=jnp.float32
    )


def head_major(rows):
    return rows.reshape(rows.shape[0], -1, HD).transpose(1, 0, 2)


def row_major(heads):
    return heads.transpose(1, 0, 2).reshape(heads.shape[1], -1)


def spread_rows(rows):
    return lax.all_gather(rows, "tp", axis=0, tiled=True)


def gather_grad(rows):
    return lax.all_gather(rows, "tp", axis=0, tiled=True)


def combine_rows(partial_value):
    return lax.psum_scatter(
        partial_value.astype(jnp.bfloat16), "tp", scatter_dimension=0, tiled=True
    ).astype(jnp.float32)


def combine_grads(partial_value):
    return lax.psum_scatter(
        partial_value.astype(jnp.bfloat16), "tp", scatter_dimension=0, tiled=True
    ).astype(jnp.float32)


def fetch(params, layer_id):
    (
        first_gain,
        first_shift,
        joint_weight,
        query_bias,
        value_bias,
        out_weight,
        out_bias,
        second_gain,
        second_shift,
        expand_weight,
        expand_bias,
        reduce_weight,
        reduce_bias,
    ) = params
    return (
        lax.all_gather(first_gain[layer_id], "fsdp", axis=0, tiled=True),
        lax.all_gather(first_shift[layer_id], "fsdp", axis=0, tiled=True),
        lax.all_gather(joint_weight[layer_id], "fsdp", axis=0, tiled=True),
        lax.all_gather(query_bias[layer_id], "fsdp", axis=1, tiled=True),
        lax.all_gather(value_bias[layer_id], "fsdp", axis=1, tiled=True),
        lax.all_gather(out_weight[layer_id], "fsdp", axis=1, tiled=True),
        lax.all_gather(out_bias[layer_id], "fsdp", axis=0, tiled=True),
        lax.all_gather(second_gain[layer_id], "fsdp", axis=0, tiled=True),
        lax.all_gather(second_shift[layer_id], "fsdp", axis=0, tiled=True),
        lax.all_gather(expand_weight[layer_id], "fsdp", axis=0, tiled=True),
        lax.all_gather(expand_bias[layer_id], "fsdp", axis=1, tiled=True),
        lax.all_gather(reduce_weight[layer_id], "fsdp", axis=1, tiled=True),
        lax.all_gather(reduce_bias[layer_id], "fsdp", axis=0, tiled=True),
    )


def attention_scores(query_heads, key_heads, key_bias):
    raw_scores = jnp.einsum(
        "hqd,hkd->hqk", query_heads, key_heads, preferred_element_type=jnp.float32
    )
    return raw_scores * HD ** (-0.5) + key_bias


def forward_layer(residual, layer_weights, key_bias):
    (
        gain_attn,
        shift_attn,
        joint_mat,
        query_add,
        value_add,
        out_mat,
        out_add,
        gain_mlp,
        shift_mlp,
        expand_mat,
        expand_add,
        reduce_mat,
        reduce_add,
    ) = layer_weights
    normed = norm_rows(residual, gain_attn.astype(jnp.float32), shift_attn.astype(jnp.float32))
    first_in = spread_rows(normed.astype(jnp.bfloat16))
    joint = jnp.einsum("nd,dce->nce", first_in, joint_mat, preferred_element_type=jnp.float32)
    queries = (joint[:, 0] + query_add.reshape(-1).astype(jnp.float32)).astype(jnp.bfloat16)
    keys_local = joint[:, 1].astype(jnp.bfloat16)
    values_local = (joint[:, 2] + value_add.reshape(-1).astype(jnp.float32)).astype(jnp.bfloat16)
    keys_all, values_all = (
        lax.all_gather(keys_local, "ctx", axis=0, tiled=True),
        lax.all_gather(values_local, "ctx", axis=0, tiled=True),
    )
    query_heads = head_major(queries)
    key_heads = head_major(keys_all)
    value_heads = head_major(values_all)
    scores = attention_scores(query_heads, key_heads, key_bias)
    row_top = jnp.max(scores, axis=-1, keepdims=True)
    exponent = jnp.exp(scores - row_top)
    row_total = jnp.sum(exponent, axis=-1, keepdims=True)
    probs_low = (exponent / row_total).astype(jnp.bfloat16)
    log_total = row_top + jnp.log(row_total)
    mixed_heads = jnp.einsum(
        "hqk,hkd->hqd", probs_low, value_heads, preferred_element_type=jnp.float32
    )
    mixed = row_major(mixed_heads.astype(jnp.bfloat16))
    middle = residual + (combine_rows(dense(mixed, out_mat)) + out_add.astype(jnp.float32))
    normed_mlp = norm_rows(middle, gain_mlp.astype(jnp.float32), shift_mlp.astype(jnp.float32))
    second_in = spread_rows(normed_mlp.astype(jnp.bfloat16))
    before = dense(second_in, expand_mat) + expand_add.reshape(-1).astype(jnp.float32)
    active = exact_gelu(before).astype(jnp.bfloat16)
    result = middle + (combine_rows(dense(active, reduce_mat)) + reduce_add.astype(jnp.float32))
    stored = (
        residual,
        first_in,
        query_heads,
        key_heads,
        value_heads,
        log_total,
        mixed,
        middle,
        second_in,
        before,
        active,
    )
    return (result, stored)


def backward_layer(carry, stored, layer_weights, key_bias):
    (
        gain_attn,
        shift_attn,
        joint_mat,
        query_add,
        value_add,
        out_mat,
        out_add,
        gain_mlp,
        shift_mlp,
        expand_mat,
        expand_add,
        reduce_mat,
        reduce_add,
    ) = layer_weights
    (
        residual,
        first_in,
        query_heads,
        key_heads,
        value_heads,
        log_total,
        mixed,
        middle,
        second_in,
        before,
        active,
    ) = stored
    low_mlp = carry.astype(jnp.bfloat16)
    mlp_rows = gather_grad(low_mlp)
    d_reduce_mat = dense_left(active, mlp_rows)
    d_reduce_add = jnp.sum(low_mlp.astype(jnp.float32), axis=0)
    d_active = dense_right(mlp_rows, reduce_mat)
    gelu_value, gelu_back = jax.vjp(exact_gelu, before)
    d_before = gelu_back(d_active)[0].astype(jnp.bfloat16)
    d_expand_add = jnp.sum(d_before.astype(jnp.float32), axis=0).reshape(expand_add.shape)
    d_expand_mat = dense_left(second_in, d_before)
    d_second = combine_grads(dense_right(d_before, expand_mat))
    norm_value, norm_back = jax.vjp(
        norm_rows, middle, gain_mlp.astype(jnp.float32), shift_mlp.astype(jnp.float32)
    )
    d_middle, d_gain_mlp, d_shift_mlp = norm_back(d_second)
    carry_mid = carry + d_middle
    low_attn = carry_mid.astype(jnp.bfloat16)
    attn_rows = gather_grad(low_attn)
    d_out_mat = dense_left(mixed, attn_rows)
    d_out_add = jnp.sum(low_attn.astype(jnp.float32), axis=0)
    d_mixed = head_major(dense_right(attn_rows, out_mat).astype(jnp.bfloat16))
    scores = attention_scores(query_heads, key_heads, key_bias)
    attn_probs = jnp.exp(scores - log_total)
    d_values = jnp.einsum(
        "hqk,hqd->hkd", attn_probs.astype(jnp.bfloat16), d_mixed, preferred_element_type=jnp.float32
    )
    d_probs = jnp.einsum("hqd,hkd->hqk", d_mixed, value_heads, preferred_element_type=jnp.float32)
    d_scores = attn_probs * (d_probs - jnp.sum(attn_probs * d_probs, axis=-1, keepdims=True))
    d_raw = (d_scores * HD ** (-0.5)).astype(jnp.bfloat16)
    d_queries = jnp.einsum("hqk,hkd->hqd", d_raw, key_heads, preferred_element_type=jnp.float32)
    d_queries = row_major(d_queries.astype(jnp.bfloat16))
    d_keys = jnp.einsum("hqk,hqd->hkd", d_raw, query_heads, preferred_element_type=jnp.float32)
    d_keys = row_major(d_keys)
    d_values = row_major(d_values)
    d_keys, d_values = (
        lax.psum_scatter(
            d_keys.astype(jnp.bfloat16), "ctx", scatter_dimension=0, tiled=True
        ).astype(jnp.float32),
        lax.psum_scatter(
            d_values.astype(jnp.bfloat16), "ctx", scatter_dimension=0, tiled=True
        ).astype(jnp.float32),
    )
    d_keys = d_keys.astype(jnp.bfloat16)
    d_values = d_values.astype(jnp.bfloat16)
    d_joint = jnp.stack((d_queries, d_keys, d_values), axis=1)
    d_joint_mat = jnp.einsum("nd,nce->dce", first_in, d_joint, preferred_element_type=jnp.float32)
    d_query_add = jnp.sum(d_queries.astype(jnp.float32), axis=0).reshape(query_add.shape)
    d_value_add = jnp.sum(d_values.astype(jnp.float32), axis=0).reshape(value_add.shape)
    d_first = combine_grads(
        jnp.einsum("nce,dce->nd", d_joint, joint_mat, preferred_element_type=jnp.float32)
    )
    first_value, first_back = jax.vjp(
        norm_rows, residual, gain_attn.astype(jnp.float32), shift_attn.astype(jnp.float32)
    )
    d_residual, d_gain_attn, d_shift_attn = first_back(d_first)
    carry_in = carry_mid + d_residual
    layer_grads = (
        d_gain_attn,
        d_shift_attn,
        d_joint_mat,
        d_query_add,
        d_value_add,
        d_out_mat,
        d_out_add,
        d_gain_mlp,
        d_shift_mlp,
        d_expand_mat,
        d_expand_add,
        d_reduce_mat,
        d_reduce_add,
    )
    return (carry_in, layer_grads)


def local(
    tokens,
    key_valid,
    first_gain,
    first_shift,
    joint_weight,
    query_bias,
    value_bias,
    out_weight,
    out_bias,
    second_gain,
    second_shift,
    expand_weight,
    expand_bias,
    reduce_weight,
    reduce_bias,
    cotangent,
):
    params = (
        first_gain,
        first_shift,
        joint_weight,
        query_bias,
        value_bias,
        out_weight,
        out_bias,
        second_gain,
        second_shift,
        expand_weight,
        expand_bias,
        reduce_weight,
        reduce_bias,
    )
    fetched = tuple((fetch(params, layer_id) for layer_id in range(LAYERS)))
    totals = [None] * LAYERS
    outputs = []
    row_grads = []
    for batch_id in range(MB):
        key_bias = jnp.where(key_valid[batch_id] == 1, 0.0, masked_score).astype(jnp.float32)
        residual = tokens[batch_id].astype(jnp.float32)
        stores = []
        for layer_id in range(LAYERS):
            residual, stored = forward_layer(residual, fetched[layer_id], key_bias)
            stores.append(stored)
        outputs.append(residual.astype(jnp.bfloat16))
        carry = cotangent[batch_id].astype(jnp.float32)
        for layer_id in reversed(range(LAYERS)):
            carry, layer_grads = backward_layer(
                carry, stores[layer_id], fetched[layer_id], key_bias
            )
            if totals[layer_id] is None:
                totals[layer_id] = layer_grads
            else:
                totals[layer_id] = tuple(
                    (old + new for old, new in zip(totals[layer_id], layer_grads))
                )
        row_grads.append(carry.astype(jnp.bfloat16))
    stacked = [
        jnp.stack([totals[layer_id][index] for layer_id in range(LAYERS)]) for index in range(13)
    ]
    shards = (
        lax.psum_scatter(
            stacked[0].astype(jnp.bfloat16), "fsdp", scatter_dimension=1, tiled=True
        ).astype(jnp.float32),
        lax.psum_scatter(
            stacked[1].astype(jnp.bfloat16), "fsdp", scatter_dimension=1, tiled=True
        ).astype(jnp.float32),
        lax.psum_scatter(
            stacked[2].astype(jnp.bfloat16), "fsdp", scatter_dimension=1, tiled=True
        ).astype(jnp.float32),
        lax.psum_scatter(
            stacked[3].astype(jnp.bfloat16), "fsdp", scatter_dimension=2, tiled=True
        ).astype(jnp.float32),
        lax.psum_scatter(
            stacked[4].astype(jnp.bfloat16), "fsdp", scatter_dimension=2, tiled=True
        ).astype(jnp.float32),
        lax.psum_scatter(
            stacked[5].astype(jnp.bfloat16), "fsdp", scatter_dimension=2, tiled=True
        ).astype(jnp.float32),
        lax.psum_scatter(
            stacked[6].astype(jnp.bfloat16), "fsdp", scatter_dimension=1, tiled=True
        ).astype(jnp.float32),
        lax.psum_scatter(
            stacked[7].astype(jnp.bfloat16), "fsdp", scatter_dimension=1, tiled=True
        ).astype(jnp.float32),
        lax.psum_scatter(
            stacked[8].astype(jnp.bfloat16), "fsdp", scatter_dimension=1, tiled=True
        ).astype(jnp.float32),
        lax.psum_scatter(
            stacked[9].astype(jnp.bfloat16), "fsdp", scatter_dimension=1, tiled=True
        ).astype(jnp.float32),
        lax.psum_scatter(
            stacked[10].astype(jnp.bfloat16), "fsdp", scatter_dimension=2, tiled=True
        ).astype(jnp.float32),
        lax.psum_scatter(
            stacked[11].astype(jnp.bfloat16), "fsdp", scatter_dimension=2, tiled=True
        ).astype(jnp.float32),
        lax.psum_scatter(
            stacked[12].astype(jnp.bfloat16), "fsdp", scatter_dimension=1, tiled=True
        ).astype(jnp.float32),
    )
    split_sums = (
        lax.psum(shards[2].astype(jnp.bfloat16), "ctx").astype(jnp.float32),
        lax.psum(shards[3].astype(jnp.bfloat16), "ctx").astype(jnp.float32),
        lax.psum(shards[4].astype(jnp.bfloat16), "ctx").astype(jnp.float32),
        lax.psum(shards[5].astype(jnp.bfloat16), "ctx").astype(jnp.float32),
        lax.psum(shards[9].astype(jnp.bfloat16), "ctx").astype(jnp.float32),
        lax.psum(shards[10].astype(jnp.bfloat16), "ctx").astype(jnp.float32),
        lax.psum(shards[11].astype(jnp.bfloat16), "ctx").astype(jnp.float32),
    )
    vector_part = lax.psum(
        (shards[0], shards[1], shards[6], shards[7], shards[8], shards[12]), ("ctx", "tp")
    )
    return (
        jnp.stack(outputs),
        jnp.stack(row_grads),
        vector_part[0],
        vector_part[1],
        split_sums[0],
        split_sums[1],
        split_sums[2],
        split_sums[3],
        vector_part[2],
        vector_part[3],
        vector_part[4],
        split_sums[4],
        split_sums[5],
        split_sums[6],
        vector_part[5],
    )


def solution(mesh):
    placed = (
        P("fsdp", ("ctx", "tp"), None),
        P("fsdp", None),
        P(None, "fsdp"),
        P(None, "fsdp"),
        P(None, "fsdp", None, "tp"),
        P(None, "tp", "fsdp"),
        P(None, "tp", "fsdp"),
        P(None, "tp", "fsdp"),
        P(None, "fsdp"),
        P(None, "fsdp"),
        P(None, "fsdp"),
        P(None, "fsdp", "tp"),
        P(None, "tp", "fsdp"),
        P(None, "tp", "fsdp"),
        P(None, "fsdp"),
        P("fsdp", ("ctx", "tp"), None),
    )
    return jax.shard_map(
        local,
        mesh=mesh,
        in_specs=placed,
        out_specs=(
            P("fsdp", ("ctx", "tp"), None),
            P("fsdp", ("ctx", "tp"), None),
            P(None, "fsdp"),
            P(None, "fsdp"),
            P(None, "fsdp", None, "tp"),
            P(None, "tp", "fsdp"),
            P(None, "tp", "fsdp"),
            P(None, "tp", "fsdp"),
            P(None, "fsdp"),
            P(None, "fsdp"),
            P(None, "fsdp"),
            P(None, "fsdp", "tp"),
            P(None, "tp", "fsdp"),
            P(None, "tp", "fsdp"),
            P(None, "fsdp"),
        ),
        check_vma=False,
    )
```

profile of v0, /device:TPU:0, one launch (start us, length us, event | category | flops | bytes accessed | tf_op | source)
XLA Modules:
  0.0 1841.4 jit_solution(5257562722936392963)
XLA Ops:
  240.8 27.9 %all-gather.85.cloned.1.call-done = bf16[1,1024,1024]{2,1,0:T(8,128)(2,1)} async-done(((bf16[1,256,1024]{2,1,0:T(8,128)(2,1)}), bf16[1,1024,1024]{2,1,0:T(8,128)(2,1)}) %all-gather.85.cloned.1.call-update) | async-done | bytes 2097168 | tf_op jit(solution)/shard_map/all_gather | solution.py:94
  318.6 35.0 %all-gather.87.cloned.1.call-done = bf16[1,1024,1024]{2,1,0:T(8,128)(2,1)} async-done(((bf16[1,1024,256]{2,1,0:T(8,128)(2,1)}), bf16[1,1024,1024]{2,1,0:T(8,128)(2,1)}) %all-gather.87.cloned.1.call-update) | async-done | bytes 2097168 | tf_op jit(solution)/shard_map/all_gather | solution.py:96
  388.2 20.1 %reduce-scatter.66.cloned.1.call-done = bf16[128,1024]{1,0:T(8,128)(2,1)} async-done(((bf16[512,1024]{1,0:T(8,128)(2,1)}), bf16[128,1024]{1,0:T(8,128)(2,1)}) %reduce-scatter.66.cloned.1.call-update) | async-done | bytes 262160 | tf_op jit(solution)/shard_map/reduce_scatter | solution.py:57
  597.3 27.3 %all-gather.91.cloned.1.call-done = bf16[1,1024,1024]{2,1,0:T(8,128)(2,1)} async-done(((bf16[1,256,1024]{2,1,0:T(8,128)(2,1)}), bf16[1,1024,1024]{2,1,0:T(8,128)(2,1)}) %all-gather.91.cloned.1.call-update) | async-done | bytes 2097168 | tf_op jit(solution)/shard_map/all_gather | solution.py:94
  678.8 48.4 %all-gather.93.cloned.1.call-done = bf16[1,1024,1024]{2,1,0:T(8,128)(2,1)} async-done(((bf16[1,1024,256]{2,1,0:T(8,128)(2,1)}), bf16[1,1024,1024]{2,1,0:T(8,128)(2,1)}) %all-gather.93.cloned.1.call-update) | async-done | bytes 2097168 | tf_op jit(solution)/shard_map/all_gather | solution.py:96
  771.9 26.8 %reduce-scatter.72.cloned.1.call-done = bf16[128,1024]{1,0:T(8,128)(2,1)} async-done(((bf16[512,1024]{1,0:T(8,128)(2,1)}), bf16[128,1024]{1,0:T(8,128)(2,1)}) %reduce-scatter.72.cloned.1.call-update) | async-done | bytes 262160 | tf_op jit(solution)/shard_map/reduce_scatter | solution.py:63
  800.1 26.0 %reduce-scatter.62.cloned.1.call-done = bf16[128,1024]{1,0:T(8,128)(2,1)} async-done(((bf16[512,1024]{1,0:T(8,128)(2,1)}), bf16[128,1024]{1,0:T(8,128)(2,1)}) %reduce-scatter.62.cloned.1.call-update) | async-done | bytes 262160 | tf_op jit(solution)/shard_map/reduce_scatter | solution.py:57
  826.1 27.5 %reduce-scatter.70.cloned.1.call-done = bf16[128,1024]{1,0:T(8,128)(2,1)} async-done(((bf16[512,1024]{1,0:T(8,128)(2,1)}), bf16[128,1024]{1,0:T(8,128)(2,1)}) %reduce-scatter.70.cloned.1.call-update) | async-done | bytes 262160 | tf_op jit(solution)/shard_map/reduce_scatter | solution.py:57
  881.5 23.0 %fusion.221 = bf16[4,1024,64]{1,2,0:T(8,128)(2,1)} fusion(f32[4,512,1024]{2,1,0:T(8,128)} %fusion.467, f32[4,512,1024]{2,1,0:T(8,128)} %copy-done.4, f32[4,512]{1,0:T(4,128)S(1)} %log_add_fusion.1, f32[1024]{0:T(1024)S(1)} %bitcast.661, f32[512,4,64]{0,2,1:T(8,128)S(1)} %bitcast.579, f32[4,64]{1,0:T(4,128)S(1)} %copy.126), kind=kOutput, calls=%fused_computation.234 | convolution fusion | flops 292031488 | bytes 17839104 | tf_op jit(solution)/shard_map/hqk,hqd->hkd/dot_general | solution.py:228
  921.5 22.2 %fusion.227 = bf16[4,1024,64]{1,2,0:T(8,128)(2,1)S(1)} fusion(f32[4,512,1024]{2,1,0:T(8,128)} %fusion.465, f32[4,512,1024]{2,1,0:T(8,128)} %copy-done.3, f32[4,512]{1,0:T(4,128)S(1)} %log_add_fusion.3, f32[1024]{0:T(1024)S(1)} %bitcast.649, f32[512,4,64]{0,2,1:T(8,128)S(1)} %bitcast.577, f32[4,64]{1,0:T(4,128)S(1)} %copy.126), kind=kOutput, calls=%fused_computation.236 | convolution fusion | flops 292031488 | bytes 17839104 | tf_op jit(solution)/shard_map/hqk,hqd->hkd/dot_general | solution.py:228
  951.3 21.7 %convert_reduce_fusion.26 = (f32[4,64]{1,0:T(4,128)S(1)}, bf16[4,512,64]{1,2,0:T(8,128)(2,1)S(1)}) fusion(bf16[4,1024,64]{1,2,0:T(8,128)(2,1)S(1)} %bitcast.575, f32[4,512,1024]{2,1,0:T(8,128)} %fusion.467, f32[4,512,1024]{2,1,0:T(8,128)} %copy-done.4, f32[4,512]{1,0:T(4,128)S(1)} %log_add_fusion.1, f32[1024]{0:T(1024)S(1)} %bitcast.663), kind=kOutput, calls=%fused_computation.405 | convolution fusion | flops 291900160 | bytes 17576960 | tf_op jit(solution)/shard_map/hqk,hkd->hqd/dot_general | solution.py:226
  977.0 21.7 %convert_reduce_fusion.27 = (f32[4,64]{1,0:T(4,128)S(1)}, bf16[4,512,64]{1,2,0:T(8,128)(2,1)S(1)}) fusion(bf16[4,1024,64]{1,2,0:T(8,128)(2,1)S(1)} %bitcast.573, f32[4,512,1024]{2,1,0:T(8,128)} %fusion.465, f32[4,512,1024]{2,1,0:T(8,128)} %copy-done.3, f32[4,512]{1,0:T(4,128)S(1)} %log_add_fusion.3, f32[1024]{0:T(1024)S(1)} %bitcast.651), kind=kOutput, calls=%fused_computation.406 | convolution fusion | flops 291900160 | bytes 17576960 | tf_op jit(solution)/shard_map/hqk,hkd->hqd/dot_general | solution.py:226
  1004.4 27.6 %reduce-scatter.78.cloned.1.call-done = bf16[128,1024]{1,0:T(8,128)(2,1)} async-done(((bf16[512,1024]{1,0:T(8,128)(2,1)}), bf16[128,1024]{1,0:T(8,128)(2,1)}) %reduce-scatter.78.cloned.1.call-update) | async-done | bytes 262160 | tf_op jit(solution)/shard_map/reduce_scatter | solution.py:63
  1099.8 28.2 %reduce-scatter.80.cloned.1.call-done = bf16[128,1024]{1,0:T(8,128)(2,1)} async-done(((bf16[512,1024]{1,0:T(8,128)(2,1)}), bf16[128,1024]{1,0:T(8,128)(2,1)}) %reduce-scatter.80.cloned.1.call-update) | async-done | bytes 262160 | tf_op jit(solution)/shard_map/reduce_scatter | solution.py:63
  1157.4 22.8 %fusion.218 = bf16[4,1024,64]{1,2,0:T(8,128)(2,1)} fusion(f32[4,512,1024]{2,1,0:T(8,128)} %fusion.468, f32[4,512,1024]{2,1,0:T(8,128)} %copy-done.2, f32[4,512]{1,0:T(4,128)S(1)} %log_add_fusion, f32[1024]{0:T(1024)S(1)} %bitcast.664, f32[512,4,64]{0,2,1:T(8,128)S(1)} %bitcast.569, f32[4,64]{1,0:T(4,128)S(1)} %copy-done.104), kind=kOutput, calls=%fused_computation.233 | convolution fusion | flops 292031488 | bytes 17839104 | tf_op jit(solution)/shard_map/hqk,hqd->hkd/dot_general | solution.py:228
  1196.9 22.0 %fusion.224 = bf16[4,1024,64]{1,2,0:T(8,128)(2,1)S(1)} fusion(f32[4,512,1024]{2,1,0:T(8,128)} %fusion.466, f32[4,512,1024]{2,1,0:T(8,128)} %copy-done.1, f32[4,512]{1,0:T(4,128)S(1)} %log_add_fusion.2, f32[1024]{0:T(1024)S(1)} %bitcast.652, f32[512,4,64]{0,2,1:T(8,128)S(1)} %bitcast.563, f32[4,64]{1,0:T(4,128)S(1)} %copy-done.104), kind=kOutput, calls=%fused_computation.235 | convolution fusion | flops 292031488 | bytes 17839104 | tf_op jit(solution)/shard_map/hqk,hqd->hkd/dot_general | solution.py:228
  1226.5 22.1 %convert_reduce_fusion.28 = (f32[4,64]{1,0:T(4,128)}, bf16[4,512,64]{1,2,0:T(8,128)(2,1)S(1)}) fusion(bf16[4,1024,64]{1,2,0:T(8,128)(2,1)S(1)} %bitcast.567, f32[4,512,1024]{2,1,0:T(8,128)} %fusion.468, f32[4,512,1024]{2,1,0:T(8,128)} %copy-done.2, f32[4,512]{1,0:T(4,128)S(1)} %log_add_fusion, f32[1024]{0:T(1024)S(1)} %bitcast.666), kind=kOutput, calls=%fused_computation.407 | convolution fusion | flops 291900160 | bytes 17576960 | tf_op jit(solution)/shard_map/hqk,hkd->hqd/dot_general | solution.py:226
  1252.5 22.1 %convert_reduce_fusion.29 = (f32[4,64]{1,0:T(4,128)}, bf16[4,512,64]{1,2,0:T(8,128)(2,1)S(1)}) fusion(bf16[4,1024,64]{1,2,0:T(8,128)(2,1)S(1)} %bitcast.561, f32[4,512,1024]{2,1,0:T(8,128)} %fusion.466, f32[4,512,1024]{2,1,0:T(8,128)} %copy-done.1, f32[4,512]{1,0:T(4,128)S(1)} %log_add_fusion.2, f32[1024]{0:T(1024)S(1)} %bitcast.654), kind=kOutput, calls=%fused_computation.408 | convolution fusion | flops 291900160 | bytes 17576960 | tf_op jit(solution)/shard_map/hqk,hkd->hqd/dot_general | solution.py:226
  1337.6 77.7 %reduce-scatter.110.cloned.1.call-done = bf16[2,1024,256]{2,1,0:T(8,128)(2,1)} async-done(((bf16[2,1024,1024]{2,1,0:T(8,128)(2,1)}), bf16[2,1024,256]{2,1,0:T(8,128)(2,1)}) %reduce-scatter.110.cloned.1.call-update) | async-done | bytes 1048592 | tf_op jit(solution)/shard_map/reduce_scatter | solution.py:365
  1415.3 79.5 %reduce-scatter.108.cloned.1.call-done = bf16[2,256,1024]{2,1,0:T(8,128)(2,1)} async-done(((bf16[2,1024,1024]{2,1,0:T(8,128)(2,1)}), bf16[2,256,1024]{2,1,0:T(8,128)(2,1)}) %reduce-scatter.108.cloned.1.call-update) | async-done | bytes 1048592 | tf_op jit(solution)/shard_map/reduce_scatter | solution.py:359
  1494.7 63.2 %reduce-scatter.104.cloned.1.call-done = bf16[2,256,3,256]{3,1,2,0:T(8,128)(2,1)} async-done(((bf16[2,1024,3,256]{3,1,2,0:T(8,128)(2,1)}), bf16[2,256,3,256]{3,1,2,0:T(8,128)(2,1)}) %reduce-scatter.104.cloned.1.call-update) | async-done | bytes 786448 | tf_op jit(solution)/shard_map/reduce_scatter | solution.py:338
  1559.9 19.9 %reduce-scatter.128.cloned.1.call-done = bf16[256,2]{1,0:T(8,128)(2,1)} async-done(((bf16[1024,2]{1,0:T(8,128)(2,1)}), bf16[256,2]{1,0:T(8,128)(2,1)}) %reduce-scatter.128.cloned.1.call-update) | async-done | bytes 1040
  1741.2 22.8 %all-reduce = (f32[2,256]{1,0:T(2,128)}, f32[2,256]{1,0:T(2,128)}, f32[2,256]{1,0:T(2,128)}, f32[2,256]{1,0:T(2,128)}, f32[2,256]{1,0:T(2,128)}, /*index=5*/f32[2,256]{1,0:T(2,128)}) all-reduce(bf16[2,256]{1,0:T(2,128)(2,1)S(1)} %copy.164, bf16[2,256]{1,0:T(2,128)(2,1)S(1)} %copy.166, ...), channel_id=1, replica_groups=mesh['fsdp'=4,'ctx'=2,'tp'=4] {'ctx','tp'}, use_global_device_ids=true, to_apply=%region_73.74 | all-reduce | flops 3072 | bytes 18432 | tf_op jit(solution)/shard_map/psum | solution.py:381
  1764.0 63.7 %all-reduce.5.cloned.1.call-done = (bf16[2,256,3,256]{3,1,2,0:T(8,128)(2,1)}, bf16[2,256,256]{2,1,0:T(8,128)(2,1)}, bf16[2,256,1024]{2,1,0:T(8,128)(2,1)}, bf16[2,1024,256]{2,1,0:T(8,128)(2,1)}) async-done(((bf16[2,256,3,256]{3,1,2,0:T(8,128)(2,1)}, bf16[2,256,256]{2,1,0:T(8,128)(2,1)}, bf16[2,256,1024]{2,1,0:T(8,128)(2,1)}, bf16[2,1024,256]{2,1,0:T(8,128)(2,1)}), (bf16[2,256,3,256]{3,1,2,0:T(8,128)(2,1)}, ...) | async-done | bytes 3145744 | tf_op jit(solution)/shard_map/psum | solution.py:373
  (781 shorter events, 1024.4 us)
Async XLA Ops:
  34.5 112.5 %reduce-scatter.56.cloned.1.call-start = ((), (), s32[]{:S(2)}) async-start(), calls=%async_computation.38 | async-start | bytes 1310720 | tf_op jit(solution)/shard_map/reduce_scatter | solution.py:57
  225.7 127.9 %all-gather.87.cloned.1.call-start = ((), (), s32[]{:S(2)}) async-start(), calls=%async_computation.81 | async-start | bytes 2621440 | tf_op jit(solution)/shard_map/all_gather | solution.py:96
  226.9 161.3 %reduce-scatter.58.cloned.1.call-start = ((), (), s32[]{:S(2)}) async-start(), calls=%async_computation.40 | async-start | bytes 1310720 | tf_op jit(solution)/shard_map/reduce_scatter | solution.py:57
  362.7 110.7 %all-gather.67.cloned.1.call-start = ((), (), s32[]{:S(2)}) async-start(), calls=%async_computation.49 | async-start | bytes 1310720 | tf_op jit(solution)/shard_map/all_gather | solution.py:49
  411.8 164.8 %reduce-scatter.68.cloned.1.call-start = ((), (), s32[]{:S(2)}) async-start(), calls=%async_computation.50 | async-start | bytes 1310720 | tf_op jit(solution)/shard_map/reduce_scatter | solution.py:57
  582.1 145.1 %all-gather.93.cloned.1.call-start = ((), (), s32[]{:S(2)}) async-start(), calls=%async_computation.84 | async-start | bytes 2621440 | tf_op jit(solution)/shard_map/all_gather | solution.py:96
  582.8 160.9 %all-gather.95.cloned.1.call-start = ((), (), s32[]{:S(2)}) async-start(), calls=%async_computation.85 | async-start | bytes 1310720 | tf_op jit(solution)/shard_map/all_gather | solution.py:53
  583.6 188.3 %reduce-scatter.88.cloned.1.call-start = ((), (), s32[]{:S(2)}) async-start(), calls=%async_computation.64 | async-start | bytes 1310720 | tf_op jit(solution)/shard_map/reduce_scatter | solution.py:63
  760.9 113.2 %all-gather.77.cloned.1.call-start = ((), (), s32[]{:S(2)}) async-start(), calls=%async_computation.65 | async-start | bytes 1310720 | tf_op jit(solution)/shard_map/all_gather | solution.py:53
  858.0 115.2 %reduce-scatter.90.cloned.1.call-start = ((), (), s32[]{:S(2)}) async-start(), calls=%async_computation.66 | async-start | bytes 786432 | tf_op jit(solution)/shard_map/reduce_scatter | solution.py:232
  1135.2 113.6 %reduce-scatter.98.cloned.1.call-start = ((), (), s32[]{:S(2)}) async-start(), calls=%async_computation.72 | async-start | bytes 786432 | tf_op jit(solution)/shard_map/reduce_scatter | solution.py:232
  1283.2 132.0 %reduce-scatter.110.cloned.1.call-start = ((), (), s32[]{:S(2)}) async-start(), calls=%async_computation.78 | async-start | bytes 5242880 | tf_op jit(solution)/shard_map/reduce_scatter | solution.py:365
  1293.4 201.3 %reduce-scatter.108.cloned.1.call-start = ((), (), s32[]{:S(2)}) async-start(), calls=%async_computation.77 | async-start | bytes 5242880 | tf_op jit(solution)/shard_map/reduce_scatter | solution.py:359
  1303.4 254.6 %reduce-scatter.104.cloned.1.call-start = ((), (), s32[]{:S(2)}) async-start(), calls=%async_computation.75 | async-start | bytes 3932160 | tf_op jit(solution)/shard_map/reduce_scatter | solution.py:338
  1312.7 267.0 %reduce-scatter.128.cloned.1.call-start = ((), (), s32[]{:S(2)}) async-start(), calls=%async_computation.95 | async-start | bytes 327680
  1314.8 284.5 %reduce-scatter.126.cloned.1.call-start = ((), (), s32[]{:S(2)}) async-start(), calls=%async_computation.94 | async-start | bytes 20480
  1315.8 303.4 %reduce-scatter.124.cloned.1.call-start = ((), (), s32[]{:S(2)}) async-start(), calls=%async_computation.93 | async-start | bytes 327680
  1316.8 322.7 %reduce-scatter.122.cloned.1.call-start = ((), (), s32[]{:S(2)}) async-start(), calls=%async_computation.92 | async-start | bytes 327680
  1317.8 341.9 %reduce-scatter.120.cloned.1.call-start = ((), (), s32[]{:S(2)}) async-start(), calls=%async_computation.91 | async-start | bytes 327680
  1318.7 361.0 %reduce-scatter.116.cloned.1.call-start = ((), (), s32[]{:S(2)}) async-start(), calls=%async_computation.89 | async-start | bytes 20480
  1319.7 379.4 %reduce-scatter.118.cloned.1.call-start = ((), (), s32[]{:S(2)}) async-start(), calls=%async_computation.90 | async-start | bytes 20480
  1320.9 398.8 %reduce-scatter.114.cloned.1.call-start = ((), (), s32[]{:S(2)}) async-start(), calls=%async_computation.88 | async-start | bytes 327680
  1325.1 415.2 %reduce-scatter.112.cloned.1.call-start = ((), (), s32[]{:S(2)}) async-start(), calls=%async_computation.87 | async-start | bytes 327680
  1326.1 501.6 %all-reduce.5.cloned.1.call-start = ((), (), s32[]{:S(2)}) async-start(), calls=%async_computation.96 | async-start | bytes 6291456 | tf_op jit(solution)/shard_map/psum | solution.py:373
  (186 other events, 5320.8 us)
Sparse Core Ops, SparseCore 0:
  52.1 41.7 all-gather.82
  121.3 25.6 reduce-scatter.55
  195.5 24.8 reduce-scatter.63
  222.4 46.2 all-gather.84
  307.4 46.2 all-gather.86
  410.3 44.1 all-gather.88
  523.5 24.8 reduce-scatter.67
  551.5 24.9 reduce-scatter.59
  578.5 46.1 all-gather.90
  680.9 46.2 all-gather.92
  746.3 24.8 reduce-scatter.87
  773.7 24.8 reduce-scatter.71
  801.2 24.9 reduce-scatter.61
  828.7 24.8 reduce-scatter.69
  979.3 25.0 reduce-scatter.93
  1007.1 24.8 reduce-scatter.77
  1074.9 24.8 reduce-scatter.95
  1103.1 24.9 reduce-scatter.79
  1283.3 24.9 reduce-scatter.85
  1310.4 27.1 reduce-scatter.105
  1339.8 75.4 reduce-scatter.109
  1417.4 77.2 reduce-scatter.107
  1497.1 60.7 reduce-scatter.103
  1742.7 84.8 all-reduce.4
  (36 shorter events, 610.7 us)
where the time goes:
time: 1850 us; the launch traced here: 1840 us
  waiting for transfers between devices  986 us (53%)
  matrix products  382 us (21%)
  blocking collectives  331 us (18%)
  other arithmetic  66.7 us (4%)
  local copies, waits for them, and re-layouts  54.1 us (3%)
    unnamed x69, waiting for transfers between devices  168 us
    all_gather x8, waiting for transfers between devices, spread_rows(): return lax.all_gather(rows, 'tp', axis=0, tiled=True)  106 us
    reduce_scatter x8, waiting for transfers between devices, combine_grads(): lax.psum_scatter(partial_value.astype(jnp.bfloat16), 'tp', scatter_dimens...  103 us
    reduce_scatter x8, waiting for transfers between devices, combine_rows(): lax.psum_scatter(partial_value.astype(jnp.bfloat16), 'tp', scatter_dimens...  92.7 us
    dot_general x4, matrix products, backward_layer(): jnp.einsum('hqk,hqd->hkd', d_raw, query_heads, preferred_element_type=jnp...  89.9 us
    dot_general x4, matrix products, backward_layer(): jnp.einsum('hqk,hkd->hqd', d_raw, key_heads, preferred_element_type=jnp.f...  87.6 us
    all_gather x2, waiting for transfers between devices, fetch(): lax.all_gather(reduce_weight[layer_id], 'fsdp', axis=1, tiled=True)  83.4 us
    reduce_scatter x1, waiting for transfers between devices, local(): lax.psum_scatter(stacked[9].astype(jnp.bfloat16), 'fsdp', scatter_dimensi...  79.5 us
  transfers between devices with their start and end apart: 60, of which 42 were waited for; matrix products, arithmetic and copies ran while one was open for 23% of the time, Pallas kernels for 0%

commit v1 on v0

--- a/solution.py
+++ b/solution.py
@@ -370,7 +370,7 @@
         ).astype(jnp.float32),
     )
     split_sums = (
-        lax.psum(shards[2].astype(jnp.bfloat16), "ctx").astype(jnp.float32),
+        jnp.sum(lax.all_gather(shards[2].astype(jnp.bfloat16), "ctx"), axis=0).astype(jnp.float32),
         lax.psum(shards[3].astype(jnp.bfloat16), "ctx").astype(jnp.float32),
         lax.psum(shards[4].astype(jnp.bfloat16), "ctx").astype(jnp.float32),
         lax.psum(shards[5].astype(jnp.bfloat16), "ctx").astype(jnp.float32),

time: 1850 us -> 1860 us (level)
    all_gather x0 -> x1, waiting for transfers between devices: none -> 23.7 us  [local(): lax.all_gather(shards[2].astype(jnp.bfloat16), 'ctx')]
    unnamed x69 -> x70, waiting for transfers between devices: 168 us -> 168 us
  transfers between devices with their start and end apart: 60 -> 61, of which waited for: 42 -> 43; matrix products, arithmetic and copies ran while one was open for 23% -> 23% of each run, Pallas kernels for 0% -> 0%
where the time goes in v1:
time: 1860 us; the launch traced here: 1850 us
  waiting for transfers between devices  990 us (53%)
  matrix products  380 us (20%)
  blocking collectives  331 us (18%)
  other arithmetic  68.3 us (4%)
  local copies, waits for them, and re-layouts  54.3 us (3%)
    unnamed x70, waiting for transfers between devices  168 us
    all_gather x8, waiting for transfers between devices, spread_rows(): return lax.all_gather(rows, 'tp', axis=0, tiled=True)  106 us
    reduce_scatter x8, waiting for transfers between devices, combine_grads(): lax.psum_scatter(partial_value.astype(jnp.bfloat16), 'tp', scatter_dimens...  103 us
    reduce_scatter x8, waiting for transfers between devices, combine_rows(): lax.psum_scatter(partial_value.astype(jnp.bfloat16), 'tp', scatter_dimens...  92.6 us
    dot_general x4, matrix products, backward_layer(): jnp.einsum('hqk,hqd->hkd', d_raw, query_heads, preferred_element_type=jnp...  90.6 us
    dot_general x4, matrix products, backward_layer(): jnp.einsum('hqk,hkd->hqd', d_raw, key_heads, preferred_element_type=jnp.f...  86.4 us
    all_gather x2, waiting for transfers between devices, fetch(): lax.all_gather(reduce_weight[layer_id], 'fsdp', axis=1, tiled=True)  83.4 us
    reduce_scatter x1, waiting for transfers between devices, local(): lax.psum_scatter(stacked[9].astype(jnp.bfloat16), 'fsdp', scatter_dimensi...  79.5 us
  transfers between devices with their start and end apart: 61, of which 43 were waited for; matrix products, arithmetic and copies ran while one was open for 23% of the time, Pallas kernels for 0%

profile of v1, /device:TPU:0, one launch (start us, length us, event | category | flops | bytes accessed | tf_op | source)
XLA Modules:
  0.0 1846.4 jit_solution(11932278154673312541)
XLA Ops:
  240.8 27.9 %all-gather.87.cloned.1.call-done = bf16[1,1024,1024]{2,1,0:T(8,128)(2,1)} async-done(((bf16[1,256,1024]{2,1,0:T(8,128)(2,1)}), bf16[1,1024,1024]{2,1,0:T(8,128)(2,1)}) %all-gather.87.cloned.1.call-update) | async-done | bytes 2097168 | tf_op jit(solution)/shard_map/all_gather | solution.py:94
  318.6 35.0 %all-gather.89.cloned.1.call-done = bf16[1,1024,1024]{2,1,0:T(8,128)(2,1)} async-done(((bf16[1,1024,256]{2,1,0:T(8,128)(2,1)}), bf16[1,1024,1024]{2,1,0:T(8,128)(2,1)}) %all-gather.89.cloned.1.call-update) | async-done | bytes 2097168 | tf_op jit(solution)/shard_map/all_gather | solution.py:96
  388.2 20.1 %reduce-scatter.66.cloned.1.call-done = bf16[128,1024]{1,0:T(8,128)(2,1)} async-done(((bf16[512,1024]{1,0:T(8,128)(2,1)}), bf16[128,1024]{1,0:T(8,128)(2,1)}) %reduce-scatter.66.cloned.1.call-update) | async-done | bytes 262160 | tf_op jit(solution)/shard_map/reduce_scatter | solution.py:57
  597.3 27.4 %all-gather.93.cloned.1.call-done = bf16[1,1024,1024]{2,1,0:T(8,128)(2,1)} async-done(((bf16[1,256,1024]{2,1,0:T(8,128)(2,1)}), bf16[1,1024,1024]{2,1,0:T(8,128)(2,1)}) %all-gather.93.cloned.1.call-update) | async-done | bytes 2097168 | tf_op jit(solution)/shard_map/all_gather | solution.py:94
  678.8 48.4 %all-gather.95.cloned.1.call-done = bf16[1,1024,1024]{2,1,0:T(8,128)(2,1)} async-done(((bf16[1,1024,256]{2,1,0:T(8,128)(2,1)}), bf16[1,1024,1024]{2,1,0:T(8,128)(2,1)}) %all-gather.95.cloned.1.call-update) | async-done | bytes 2097168 | tf_op jit(solution)/shard_map/all_gather | solution.py:96
  771.9 26.8 %reduce-scatter.72.cloned.1.call-done = bf16[128,1024]{1,0:T(8,128)(2,1)} async-done(((bf16[512,1024]{1,0:T(8,128)(2,1)}), bf16[128,1024]{1,0:T(8,128)(2,1)}) %reduce-scatter.72.cloned.1.call-update) | async-done | bytes 262160 | tf_op jit(solution)/shard_map/reduce_scatter | solution.py:63
  800.2 26.0 %reduce-scatter.62.cloned.1.call-done = bf16[128,1024]{1,0:T(8,128)(2,1)} async-done(((bf16[512,1024]{1,0:T(8,128)(2,1)}), bf16[128,1024]{1,0:T(8,128)(2,1)}) %reduce-scatter.62.cloned.1.call-update) | async-done | bytes 262160 | tf_op jit(solution)/shard_map/reduce_scatter | solution.py:57
  826.1 27.5 %reduce-scatter.70.cloned.1.call-done = bf16[128,1024]{1,0:T(8,128)(2,1)} async-done(((bf16[512,1024]{1,0:T(8,128)(2,1)}), bf16[128,1024]{1,0:T(8,128)(2,1)}) %reduce-scatter.70.cloned.1.call-update) | async-done | bytes 262160 | tf_op jit(solution)/shard_map/reduce_scatter | solution.py:57
  881.5 22.9 %fusion.221 = bf16[4,1024,64]{1,2,0:T(8,128)(2,1)} fusion(f32[4,512,1024]{2,1,0:T(8,128)} %fusion.467, f32[4,512,1024]{2,1,0:T(8,128)} %copy-done.4, f32[4,512]{1,0:T(4,128)S(1)} %log_add_fusion.1, f32[1024]{0:T(1024)S(1)} %bitcast.663, f32[512,4,64]{0,2,1:T(8,128)S(1)} %bitcast.580, f32[4,64]{1,0:T(4,128)S(1)} %copy.126), kind=kOutput, calls=%fused_computation.234 | convolution fusion | flops 292031488 | bytes 17839104 | tf_op jit(solution)/shard_map/hqk,hqd->hkd/dot_general | solution.py:228
  921.4 22.0 %fusion.227 = bf16[4,1024,64]{1,2,0:T(8,128)(2,1)S(1)} fusion(f32[4,512,1024]{2,1,0:T(8,128)} %fusion.465, f32[4,512,1024]{2,1,0:T(8,128)} %copy-done.3, f32[4,512]{1,0:T(4,128)S(1)} %log_add_fusion.3, f32[1024]{0:T(1024)S(1)} %bitcast.651, f32[512,4,64]{0,2,1:T(8,128)S(1)} %bitcast.578, f32[4,64]{1,0:T(4,128)S(1)} %copy.126), kind=kOutput, calls=%fused_computation.236 | convolution fusion | flops 292031488 | bytes 17839104 | tf_op jit(solution)/shard_map/hqk,hqd->hkd/dot_general | solution.py:228
  951.1 21.7 %convert_reduce_fusion.26 = (f32[4,64]{1,0:T(4,128)S(1)}, bf16[4,512,64]{1,2,0:T(8,128)(2,1)S(1)}) fusion(bf16[4,1024,64]{1,2,0:T(8,128)(2,1)S(1)} %bitcast.576, f32[4,512,1024]{2,1,0:T(8,128)} %fusion.467, f32[4,512,1024]{2,1,0:T(8,128)} %copy-done.4, f32[4,512]{1,0:T(4,128)S(1)} %log_add_fusion.1, f32[1024]{0:T(1024)S(1)} %bitcast.665), kind=kOutput, calls=%fused_computation.405 | convolution fusion | flops 291900160 | bytes 17576960 | tf_op jit(solution)/shard_map/hqk,hkd->hqd/dot_general | solution.py:226
  976.8 21.5 %convert_reduce_fusion.27 = (f32[4,64]{1,0:T(4,128)S(1)}, bf16[4,512,64]{1,2,0:T(8,128)(2,1)S(1)}) fusion(bf16[4,1024,64]{1,2,0:T(8,128)(2,1)S(1)} %bitcast.574, f32[4,512,1024]{2,1,0:T(8,128)} %fusion.465, f32[4,512,1024]{2,1,0:T(8,128)} %copy-done.3, f32[4,512]{1,0:T(4,128)S(1)} %log_add_fusion.3, f32[1024]{0:T(1024)S(1)} %bitcast.653), kind=kOutput, calls=%fused_computation.406 | convolution fusion | flops 291900160 | bytes 17576960 | tf_op jit(solution)/shard_map/hqk,hkd->hqd/dot_general | solution.py:226
  1004.3 27.5 %reduce-scatter.78.cloned.1.call-done = bf16[128,1024]{1,0:T(8,128)(2,1)} async-done(((bf16[512,1024]{1,0:T(8,128)(2,1)}), bf16[128,1024]{1,0:T(8,128)(2,1)}) %reduce-scatter.78.cloned.1.call-update) | async-done | bytes 262160 | tf_op jit(solution)/shard_map/reduce_scatter | solution.py:63
  1099.7 28.2 %reduce-scatter.80.cloned.1.call-done = bf16[128,1024]{1,0:T(8,128)(2,1)} async-done(((bf16[512,1024]{1,0:T(8,128)(2,1)}), bf16[128,1024]{1,0:T(8,128)(2,1)}) %reduce-scatter.80.cloned.1.call-update) | async-done | bytes 262160 | tf_op jit(solution)/shard_map/reduce_scatter | solution.py:63
  1164.0 22.8 %fusion.218 = bf16[4,1024,64]{1,2,0:T(8,128)(2,1)} fusion(f32[4,512,1024]{2,1,0:T(8,128)} %fusion.468, f32[4,512,1024]{2,1,0:T(8,128)} %copy-done.2, f32[4,512]{1,0:T(4,128)S(1)} %log_add_fusion, f32[1024]{0:T(1024)S(1)} %bitcast.667, f32[512,4,64]{0,2,1:T(8,128)S(1)} %bitcast.570, f32[4,64]{1,0:T(4,128)S(1)} %copy-done.103), kind=kOutput, calls=%fused_computation.233 | convolution fusion | flops 292031488 | bytes 17839104 | tf_op jit(solution)/shard_map/hqk,hqd->hkd/dot_general | solution.py:228
  1201.6 22.8 %fusion.224 = bf16[4,1024,64]{1,2,0:T(8,128)(2,1)} fusion(f32[4,512,1024]{2,1,0:T(8,128)} %fusion.466, f32[4,512,1024]{2,1,0:T(8,128)} %copy-done.1, f32[4,512]{1,0:T(4,128)S(1)} %log_add_fusion.2, f32[1024]{0:T(1024)S(1)} %bitcast.655, f32[512,4,64]{0,2,1:T(8,128)S(1)} %bitcast.564, f32[4,64]{1,0:T(4,128)S(1)} %copy-done.103), kind=kOutput, calls=%fused_computation.235 | convolution fusion | flops 292031488 | bytes 17839104 | tf_op jit(solution)/shard_map/hqk,hqd->hkd/dot_general | solution.py:228
  1226.7 21.6 %convert_reduce_fusion.28 = (f32[4,64]{1,0:T(4,128)S(1)}, bf16[4,512,64]{1,2,0:T(8,128)(2,1)S(1)}) fusion(bf16[4,1024,64]{1,2,0:T(8,128)(2,1)S(1)} %bitcast.568, f32[4,512,1024]{2,1,0:T(8,128)} %fusion.468, f32[4,512,1024]{2,1,0:T(8,128)} %copy-done.2, f32[4,512]{1,0:T(4,128)S(1)} %log_add_fusion, f32[1024]{0:T(1024)S(1)} %bitcast.668), kind=kOutput, calls=%fused_computation.407 | convolution fusion | flops 291900160 | bytes 17576960 | tf_op jit(solution)/shard_map/hqk,hkd->hqd/dot_general | solution.py:226
  1252.1 21.6 %convert_reduce_fusion.29 = (f32[4,64]{1,0:T(4,128)S(1)}, bf16[4,512,64]{1,2,0:T(8,128)(2,1)S(1)}) fusion(bf16[4,1024,64]{1,2,0:T(8,128)(2,1)S(1)} %bitcast.562, f32[4,512,1024]{2,1,0:T(8,128)} %fusion.466, f32[4,512,1024]{2,1,0:T(8,128)} %copy-done.1, f32[4,512]{1,0:T(4,128)S(1)} %log_add_fusion.2, f32[1024]{0:T(1024)S(1)} %bitcast.656), kind=kOutput, calls=%fused_computation.408 | convolution fusion | flops 291900160 | bytes 17576960 | tf_op jit(solution)/shard_map/hqk,hkd->hqd/dot_general | solution.py:226
  1334.6 77.7 %reduce-scatter.110.cloned.1.call-done = bf16[2,1024,256]{2,1,0:T(8,128)(2,1)} async-done(((bf16[2,1024,1024]{2,1,0:T(8,128)(2,1)}), bf16[2,1024,256]{2,1,0:T(8,128)(2,1)}) %reduce-scatter.110.cloned.1.call-update) | async-done | bytes 1048592 | tf_op jit(solution)/shard_map/reduce_scatter | solution.py:365
  1412.3 79.5 %reduce-scatter.108.cloned.1.call-done = bf16[2,256,1024]{2,1,0:T(8,128)(2,1)} async-done(((bf16[2,1024,1024]{2,1,0:T(8,128)(2,1)}), bf16[2,256,1024]{2,1,0:T(8,128)(2,1)}) %reduce-scatter.108.cloned.1.call-update) | async-done | bytes 1048592 | tf_op jit(solution)/shard_map/reduce_scatter | solution.py:359
  1491.8 63.1 %reduce-scatter.104.cloned.1.call-done = bf16[2,256,3,256]{3,1,2,0:T(8,128)(2,1)} async-done(((bf16[2,1024,3,256]{3,1,2,0:T(8,128)(2,1)}), bf16[2,256,3,256]{3,1,2,0:T(8,128)(2,1)}) %reduce-scatter.104.cloned.1.call-update) | async-done | bytes 786448 | tf_op jit(solution)/shard_map/reduce_scatter | solution.py:338
  1738.2 22.8 %all-reduce = (f32[2,256]{1,0:T(2,128)}, f32[2,256]{1,0:T(2,128)}, f32[2,256]{1,0:T(2,128)}, f32[2,256]{1,0:T(2,128)}, f32[2,256]{1,0:T(2,128)}, /*index=5*/f32[2,256]{1,0:T(2,128)}) all-reduce(bf16[2,256]{1,0:T(2,128)(2,1)S(1)} %copy.164, bf16[2,256]{1,0:T(2,128)(2,1)S(1)} %copy.166, ...), channel_id=1, replica_groups=mesh['fsdp'=4,'ctx'=2,'tp'=4] {'ctx','tp'}, use_global_device_ids=true, to_apply=%region_73.74 | all-reduce | flops 3072 | bytes 18432 | tf_op jit(solution)/shard_map/psum | solution.py:381
  1761.0 46.3 %all-reduce.5.cloned.1.call-done = (bf16[2,256,256]{2,1,0:T(8,128)(2,1)}, bf16[2,256,1024]{2,1,0:T(8,128)(2,1)}, bf16[2,1024,256]{2,1,0:T(8,128)(2,1)}) async-done(((bf16[2,256,256]{2,1,0:T(8,128)(2,1)}, bf16[2,256,1024]{2,1,0:T(8,128)(2,1)}, bf16[2,1024,256]{2,1,0:T(8,128)(2,1)}), (bf16[2,256,256]{2,1,0:T(8,128)(2,1)}, bf16[2,256,1024]{2,1,0:T(8,128)(2,1)}, ...) | async-done | bytes 2359312 | tf_op jit(solution)/shard_map/psum | solution.py:376
  1812.4 23.7 %all-gather.101.cloned.1.call-done = bf16[4,256,3,256]{3,1,2,0:T(8,128)(2,1)} async-done(((bf16[2,256,3,256]{3,1,2,0:T(8,128)(2,1)}), bf16[4,256,3,256]{3,1,2,0:T(8,128)(2,1)}) %all-gather.101.cloned.1.call-update) | async-done | bytes 1572880 | tf_op jit(solution)/shard_map/all_gather | solution.py:373
  (779 shorter events, 1043.9 us)
Async XLA Ops:
  34.5 112.5 %reduce-scatter.56.cloned.1.call-start = ((), (), s32[]{:S(2)}) async-start(), calls=%async_computation.38 | async-start | bytes 1310720 | tf_op jit(solution)/shard_map/reduce_scatter | solution.py:57
  225.7 127.9 %all-gather.89.cloned.1.call-start = ((), (), s32[]{:S(2)}) async-start(), calls=%async_computation.81 | async-start | bytes 2621440 | tf_op jit(solution)/shard_map/all_gather | solution.py:96
  226.9 161.3 %reduce-scatter.58.cloned.1.call-start = ((), (), s32[]{:S(2)}) async-start(), calls=%async_computation.40 | async-start | bytes 1310720 | tf_op jit(solution)/shard_map/reduce_scatter | solution.py:57
  411.8 164.8 %reduce-scatter.68.cloned.1.call-start = ((), (), s32[]{:S(2)}) async-start(), calls=%async_computation.50 | async-start | bytes 1310720 | tf_op jit(solution)/shard_map/reduce_scatter | solution.py:57
  582.1 145.1 %all-gather.95.cloned.1.call-start = ((), (), s32[]{:S(2)}) async-start(), calls=%async_computation.84 | async-start | bytes 2621440 | tf_op jit(solution)/shard_map/all_gather | solution.py:96
  582.8 160.9 %all-gather.97.cloned.1.call-start = ((), (), s32[]{:S(2)}) async-start(), calls=%async_computation.85 | async-start | bytes 1310720 | tf_op jit(solution)/shard_map/all_gather | solution.py:53
  583.6 188.4 %reduce-scatter.88.cloned.1.call-start = ((), (), s32[]{:S(2)}) async-start(), calls=%async_computation.64 | async-start | bytes 1310720 | tf_op jit(solution)/shard_map/reduce_scatter | solution.py:63
  761.0 113.2 %all-gather.79.cloned.1.call-start = ((), (), s32[]{:S(2)}) async-start(), calls=%async_computation.65 | async-start | bytes 1310720 | tf_op jit(solution)/shard_map/all_gather | solution.py:53
  858.0 115.0 %reduce-scatter.90.cloned.1.call-start = ((), (), s32[]{:S(2)}) async-start(), calls=%async_computation.66 | async-start | bytes 786432 | tf_op jit(solution)/shard_map/reduce_scatter | solution.py:232
  1135.0 113.4 %reduce-scatter.100.cloned.1.call-start = ((), (), s32[]{:S(2)}) async-start(), calls=%async_computation.73 | async-start | bytes 786432 | tf_op jit(solution)/shard_map/reduce_scatter | solution.py:235
  1282.4 129.9 %reduce-scatter.110.cloned.1.call-start = ((), (), s32[]{:S(2)}) async-start(), calls=%async_computation.78 | async-start | bytes 5242880 | tf_op jit(solution)/shard_map/reduce_scatter | solution.py:365
  1292.6 199.1 %reduce-scatter.108.cloned.1.call-start = ((), (), s32[]{:S(2)}) async-start(), calls=%async_computation.77 | async-start | bytes 5242880 | tf_op jit(solution)/shard_map/reduce_scatter | solution.py:359
  1302.7 252.2 %reduce-scatter.104.cloned.1.call-start = ((), (), s32[]{:S(2)}) async-start(), calls=%async_computation.75 | async-start | bytes 3932160 | tf_op jit(solution)/shard_map/reduce_scatter | solution.py:338
  1312.1 264.8 %reduce-scatter.128.cloned.1.call-start = ((), (), s32[]{:S(2)}) async-start(), calls=%async_computation.96 | async-start | bytes 327680
  1314.1 282.1 %reduce-scatter.126.cloned.1.call-start = ((), (), s32[]{:S(2)}) async-start(), calls=%async_computation.95 | async-start | bytes 20480
  1315.1 301.1 %reduce-scatter.124.cloned.1.call-start = ((), (), s32[]{:S(2)}) async-start(), calls=%async_computation.94 | async-start | bytes 327680
  1316.1 320.3 %reduce-scatter.122.cloned.1.call-start = ((), (), s32[]{:S(2)}) async-start(), calls=%async_computation.93 | async-start | bytes 327680
  1317.1 339.6 %reduce-scatter.120.cloned.1.call-start = ((), (), s32[]{:S(2)}) async-start(), calls=%async_computation.92 | async-start | bytes 327680
  1318.1 358.6 %reduce-scatter.116.cloned.1.call-start = ((), (), s32[]{:S(2)}) async-start(), calls=%async_computation.90 | async-start | bytes 20480
  1319.0 377.0 %reduce-scatter.118.cloned.1.call-start = ((), (), s32[]{:S(2)}) async-start(), calls=%async_computation.91 | async-start | bytes 20480
  1320.2 396.4 %reduce-scatter.114.cloned.1.call-start = ((), (), s32[]{:S(2)}) async-start(), calls=%async_computation.89 | async-start | bytes 327680
  1324.4 412.9 %reduce-scatter.112.cloned.1.call-start = ((), (), s32[]{:S(2)}) async-start(), calls=%async_computation.88 | async-start | bytes 327680
  1325.4 481.8 %all-reduce.5.cloned.1.call-start = ((), (), s32[]{:S(2)}) async-start(), calls=%async_computation.97 | async-start | bytes 4718592 | tf_op jit(solution)/shard_map/psum | solution.py:376
  1491.8 344.3 %all-gather.101.cloned.1.call-start = ((), (), s32[]{:S(2)}) async-start(), calls=%async_computation.87 | async-start | bytes 2359296 | tf_op jit(solution)/shard_map/all_gather | solution.py:373
  (184 other events, 5763.1 us)
Sparse Core Ops, SparseCore 0:
  52.1 41.7 all-gather.84
  121.3 25.6 reduce-scatter.55
  195.5 24.8 reduce-scatter.63
  222.4 46.2 all-gather.86
  307.4 46.2 all-gather.88
  410.3 44.1 all-gather.90
  551.5 24.9 reduce-scatter.59
  578.5 46.1 all-gather.92
  680.9 46.2 all-gather.94
  746.3 24.8 reduce-scatter.87
  773.8 24.8 reduce-scatter.71
  801.2 24.8 reduce-scatter.61
  828.7 24.8 reduce-scatter.69
  979.1 25.1 reduce-scatter.93
  1074.7 24.8 reduce-scatter.95
  1102.9 24.8 reduce-scatter.79
  1252.2 24.9 reduce-scatter.101
  1280.3 24.9 reduce-scatter.85
  1307.4 27.1 reduce-scatter.105
  1336.8 75.4 reduce-scatter.109
  1414.4 77.2 reduce-scatter.107
  1494.1 60.7 reduce-scatter.103
  1739.7 67.4 all-reduce.4
  1808.9 27.2 all-gather.100
  (37 shorter events, 635.3 us)
